TPU v7x, 128 devices: a whole 4x4x4 slice. The times are simulated.
128 devices in a mesh: tok: 32 (over y, x, core), mlp: 4 (over z).
Axes of the slice: x: 4, y: 4, z: 4, core: 2. Of those that a mesh axis runs over, the one named last changes fastest.
Arguments:
- layer_input: bfloat16 [16384, 4096], P('tok'), may hold values from -80 to 80
- input_norm_gain: float32 [4096], replicated, may hold values from 0.6 to 10
- query_weight: bfloat16 [4096, 4096], P(None, 'mlp'), may hold values from -0.09375 to 0.09375
- key_weight: bfloat16 [4096, 1024], P(None, 'mlp'), may hold values from -0.09375 to 0.09375
- value_weight: bfloat16 [4096, 1024], P(None, 'mlp'), may hold values from -0.09375 to 0.09375
- query_down_maps: bfloat16 [256, 16, 4096], P('tok', None, 'mlp'), may hold values from -0.09375 to 0.09375
- value_down_maps: bfloat16 [256, 16, 4096], P('tok', None, 'mlp'), may hold values from -0.09375 to 0.09375
- query_up_maps: bfloat16 [256, 16, 4096], P('tok', None, 'mlp'), may hold values from -1.5 to 1.5
- value_up_maps: bfloat16 [256, 16, 1024], P('tok', None, 'mlp'), may hold values from -1.5 to 1.5
- tenant_prompt_length: int32 [16], replicated, may hold values from 1 to 2048, 16384 in all
- tenant_adapter_id: int32 [16], replicated, may hold values from 0 to 255
- adapter_storage_slot: int32 [256], replicated, may hold values from 0 to 255, each once
Outputs:
- attended: bfloat16 [16384, 4096], P('tok', 'mlp')
Inputs may be any that keep to these rules, and one draw needn't show every extreme that they name: `tenant_prompt_length`: the lengths sum to 16384; each is at most 2048 and one of them is exactly that. `tenant_adapter_id`: tenants may share an adapter. `adapter_storage_slot`: each storage slot holds exactly one adapter.
All inputs are finite; a program needn't handle non-finite values.
Results may differ from a plain program's by a relative error of at most 0.0045.
The roundings to bfloat16 on the way count: a program that leaves them out, or rounds other values in their place, can miss the bound.
Values may be sent and summed in bfloat16 or wider, within the bound.
A program may use at most 192 MiB of HBM per device.

v0:
```python
import jax
import jax.numpy as jnp
from jax import lax
from jax.sharding import PartitionSpec as P

HEAD_WIDTH = 128
ADAPTER_RANK = 16
LONGEST_PROMPT = 4
NORM_EPS = 1e-05
ROPE_BASE = 500000.0
ADAPTER_SCALE = 0.5


def from_behind(x, axis, by):
    peers = lax.axis_size(axis)
    pairs = [(i, i + by) for i in range(peers) if 0 <= i + by < peers]
    return lax.ppermute(x, axis, pairs)


def rotary(values, positions):
    half_width = values.shape[-1] // 2
    exponent = jnp.arange(half_width).astype(jnp.float32) * (2.0 / values.shape[-1])
    inverse = jnp.exp(-exponent * jnp.log(jnp.float32(ROPE_BASE)))
    angles = positions.astype(jnp.float32)[:, None] * inverse[None, :]
    cosine = jnp.cos(angles)[:, None, :]
    sine = jnp.sin(angles)[:, None, :]
    first_position = values[..., :half_width]
    second = values[..., half_width:]
    return jnp.concatenate(
        [first_position * cosine - second * sine, second * cosine + first_position * sine], axis=-1
    )


def tenant_of(tenant_prompt_length, indices):
    prompt_ends = jnp.cumsum(tenant_prompt_length)
    prompt_starts = prompt_ends - tenant_prompt_length
    tenant_ids = jnp.sum((indices[:, None] >= prompt_ends[None, :]).astype(jnp.int32), axis=1)
    member = (
        tenant_ids[:, None] == jnp.arange(tenant_prompt_length.shape[0], dtype=jnp.int32)[None, :]
    )
    row_start = jnp.sum(jnp.where(member, prompt_starts[None, :], 0), axis=1)
    return (member, row_start)


def contract(left, table):
    flat = table.reshape(-1, table.shape[2])
    return lax.dot_general(left, flat, (((1,), (1,)), ((), ())), preferred_element_type=jnp.float32)


def body(
    layer_input,
    input_norm_gain,
    query_weight,
    key_weight,
    value_weight,
    query_down_maps,
    value_down_maps,
    query_up_maps,
    value_up_maps,
    tenant_prompt_length,
    tenant_adapter_id,
    adapter_storage_slot,
):
    tok_rows = layer_input.shape[0]
    device = lax.axis_index("tok")
    held_tokens = query_down_maps.shape[0]
    catalog = adapter_storage_slot.shape[0]
    matches = tenant_adapter_id[:, None] == jnp.arange(catalog, dtype=jnp.int32)[None, :]
    storage_slots = jnp.sum(jnp.where(matches, adapter_storage_slot[None, :], 0), axis=1)
    local_slot = storage_slots - device * held_tokens
    picker = (local_slot[:, None] == jnp.arange(held_tokens, dtype=jnp.int32)[None, :]).astype(
        jnp.bfloat16
    )

    def selector(stored):
        return jnp.einsum("th,hrc->trc", picker, stored, preferred_element_type=jnp.float32)

    summed = (
        lax.psum(selector(query_down_maps).astype(jnp.bfloat16), "tok").astype(jnp.float32),
        lax.psum(selector(value_down_maps).astype(jnp.bfloat16), "tok").astype(jnp.float32),
        lax.psum(selector(query_up_maps).astype(jnp.bfloat16), "tok").astype(jnp.float32),
        lax.psum(selector(value_up_maps).astype(jnp.bfloat16), "tok").astype(jnp.float32),
    )
    query_down_table = summed[0].astype(jnp.bfloat16)
    value_down_table = summed[1].astype(jnp.bfloat16)
    query_up_table = summed[2].astype(jnp.bfloat16)
    value_up_table = summed[3].astype(jnp.bfloat16)
    widened = layer_input.astype(jnp.float32)
    scale_row = lax.rsqrt(jnp.mean(widened * widened, axis=1, keepdims=True) + NORM_EPS)
    normed_input = (widened * scale_row * input_norm_gain[None, :]).astype(jnp.bfloat16)
    indices = device * tok_rows + jnp.arange(tok_rows, dtype=jnp.int32)
    member, row_start = tenant_of(tenant_prompt_length, indices)
    positions = indices - row_start
    chosen = jnp.repeat(member, ADAPTER_RANK, axis=1)
    full_aq, full_av = (
        lax.all_gather(query_down_table, "mlp", axis=2, tiled=True),
        lax.all_gather(value_down_table, "mlp", axis=2, tiled=True),
    )
    shrink_q = contract(normed_input, full_aq)
    shrink_v = contract(normed_input, full_av)
    shrink_q = jnp.where(chosen, shrink_q, 0.0).astype(jnp.bfloat16)
    shrink_v = jnp.where(chosen, shrink_v, 0.0).astype(jnp.bfloat16)
    query_delta = jnp.dot(
        shrink_q,
        query_up_table.reshape(-1, query_up_table.shape[2]),
        preferred_element_type=jnp.float32,
    )
    value_delta = jnp.dot(
        shrink_v,
        value_up_table.reshape(-1, value_up_table.shape[2]),
        preferred_element_type=jnp.float32,
    )
    query_rows = (
        jnp.dot(normed_input, query_weight, preferred_element_type=jnp.float32)
        + ADAPTER_SCALE * query_delta
    )
    query_rows = rotary(query_rows.reshape(tok_rows, -1, HEAD_WIDTH), positions).astype(
        jnp.bfloat16
    )
    key = jnp.dot(normed_input, key_weight, preferred_element_type=jnp.float32)
    key = rotary(key.reshape(tok_rows, -1, HEAD_WIDTH), positions).astype(jnp.bfloat16)
    value_rows = (
        jnp.dot(normed_input, value_weight, preferred_element_type=jnp.float32)
        + ADAPTER_SCALE * value_delta
    )
    value_rows = value_rows.astype(jnp.bfloat16).reshape(tok_rows, -1, HEAD_WIDTH)
    key_blocks = []
    value_blocks = []
    for shift_by in range(LONGEST_PROMPT, 0, -1):
        moved_key, moved_value = from_behind((key, value_rows), "tok", shift_by)
        key_blocks.append(moved_key)
        value_blocks.append(moved_value)
    key_blocks.append(key)
    value_blocks.append(value_rows)
    all_values = jnp.concatenate(value_blocks, axis=0)
    span = (LONGEST_PROMPT + 1) * tok_rows
    k_index = (device - LONGEST_PROMPT) * tok_rows + jnp.arange(span, dtype=jnp.int32)
    allowed = (k_index[None, :] >= row_start[:, None]) & (k_index[None, :] <= indices[:, None])
    heads_here = query_rows.shape[1]
    kv_here = key.shape[1]
    head_groups = heads_here // kv_here
    outputs = []
    for kv_group in range(kv_here):
        q_group = query_rows[:, kv_group * head_groups : (kv_group + 1) * head_groups, :]
        pieces = []
        for block_index in range(LONGEST_PROMPT + 1):
            block_keys = key_blocks[block_index][:, kv_group, :]

            def dense_scores(q_group=q_group, block_keys=block_keys):
                return jnp.einsum(
                    "qgd,kd->gqk", q_group, block_keys, preferred_element_type=jnp.float32
                )

            pieces.append(dense_scores())
        scores = jnp.concatenate(pieces, axis=2) * HEAD_WIDTH ** (-0.5)
        scores = jnp.where(allowed[None], scores, -jnp.inf)
        peak = jnp.max(scores, axis=-1, keepdims=True)
        weights = jnp.exp(scores - peak)
        totals = jnp.sum(weights, axis=-1)
        probs = weights.astype(jnp.bfloat16)
        mixed = jnp.einsum(
            "gqk,kd->qgd", probs, all_values[:, kv_group, :], preferred_element_type=jnp.float32
        )
        outputs.append(mixed / jnp.transpose(totals)[:, :, None])
    attended = jnp.concatenate(outputs, axis=1).astype(jnp.bfloat16)
    return attended.reshape(tok_rows, heads_here * HEAD_WIDTH)


def solution(mesh):
    placed = (
        P("tok", None),
        P(),
        P(None, "mlp"),
        P(None, "mlp"),
        P(None, "mlp"),
        P("tok", None, "mlp"),
        P("tok", None, "mlp"),
        P("tok", None, "mlp"),
        P("tok", None, "mlp"),
        P(),
        P(),
        P(),
    )
    return jax.shard_map(
        body, mesh=mesh, in_specs=placed, out_specs=P("tok", "mlp"), check_vma=False
    )
```

profile of v0, /device:TPU:1, one launch (start us, length us, event | category | flops | bytes accessed | tf_op | source)
XLA Modules:
  0.0 289.7 jit_solution(7563186682735671526)
XLA Ops:
  16.3 3.1 %fusion.12 = f32[512]{0:T(512)S(1)} fusion(bf16[512,4096]{1,0:T(8,128)(2,1)} %param.12), kind=kLoop, calls=%fused_computation.16 | loop fusion | flops 6290944 | bytes 4196352 | tf_op jit(solution)/shard_map/reduce_sum | solution.py:89
  19.4 106.0 %all-reduce.3.cloned.1.call-done = (bf16[256,1024]{1,0:T(8,128)(2,1)}, bf16[16,16,1024]{2,0,1:T(8,128)(2,1)}, bf16[256,256]{1,0:T(8,128)(2,1)}, bf16[16,16,1024]{2,0,1:T(8,128)(2,1)}) async-done(((bf16[256,1024]{1,0:T(8,128)(2,1)}, bf16[16,16,1024]{2,0,1:T(8,128)(2,1)}, bf16[256,256]{1,0:T(8,128)(2,1)}, bf16[16,16,1024]{2,0,1:T(8,128)(2,1)}), (bf16[256,1024]{1,0:T(8,128)(2,1)}, ...) | async-done | bytes 1703952 | tf_op jit(solution)/shard_map/psum | solution.py:81
  125.5 3.8 %fusion.14 = bf16[512,4096]{1,0:T(8,128)(2,1)S(1)} fusion(bf16[512,4096]{1,0:T(8,128)(2,1)} %param.12, f32[4096]{0:T(1024)S(1)} %copy-done.15, f32[512]{0:T(512)S(1)} %add_rsqrt_fusion), kind=kLoop, calls=%fused_computation.18 | loop fusion | flops 8388608 | bytes 8407040 | tf_op jit(solution)/shard_map/convert_element_type | solution.py:90
  136.0 3.1 %collective-permute-start.7 = (bf16[512,2,128]{2,0,1:T(8,128)(2,1)}, bf16[512,2,128]{2,0,1:T(8,128)(2,1)}, u32[]{:S(2)}, u32[]{:S(2)}) collective-permute-start(bf16[512,2,128]{2,0,1:T(8,128)(2,1)} %pad_maximum_fusion.2), channel_id=1, source_target_pairs={{0,4},{4,8},{8,12},{12,16},{16,20},{20,24},{24,28},{28,32},{32,36}... | collective-permute-start | bytes 786440 | tf_op jit(solution)/shard_map/ppermute | solution.py:17
  139.1 3.8 %collective-permute-start.6 = (bf16[512,2,128]{2,0,1:T(8,128)(2,1)}, bf16[512,2,128]{2,0,1:T(8,128)(2,1)}, u32[]{:S(2)}, u32[]{:S(2)}) collective-permute-start(bf16[512,2,128]{2,0,1:T(8,128)(2,1)} %pad_maximum_fusion.2), channel_id=1, source_target_pairs={{0,8},{4,12},{8,16},{12,20},{16,24},{20,28},{24,32},{28,36},{32,40... | collective-permute-start | bytes 786440 | tf_op jit(solution)/shard_map/ppermute | solution.py:17
  142.9 4.9 %collective-permute-start.5 = (bf16[512,2,128]{2,0,1:T(8,128)(2,1)}, bf16[512,2,128]{2,0,1:T(8,128)(2,1)}, u32[]{:S(2)}, u32[]{:S(2)}) collective-permute-start(bf16[512,2,128]{2,0,1:T(8,128)(2,1)} %pad_maximum_fusion.2), channel_id=1, source_target_pairs={{0,12},{4,16},{8,20},{12,24},{16,28},{20,32},{24,36},{28,40},{32,4... | collective-permute-start | bytes 786440 | tf_op jit(solution)/shard_map/ppermute | solution.py:17
  150.2 5.1 %fusion.61 = f32[512,256]{0,1:T(8,128)} fusion(bf16[512,4096]{1,0:T(8,128)(2,1)} %copy-done.2, bf16[4096,256]{1,0:T(8,128)(2,1)} %param.16), kind=kOutput, calls=%fused_computation.114 | convolution fusion | flops 1073741824 | bytes 6815744 | tf_op jit(solution)/shard_map/dot_general | solution.py:123
  156.7 8.3 %fusion.63 = f32[512,1024]{1,0:T(8,128)} fusion(bf16[512,4096]{1,0:T(8,128)(2,1)S(1)} %copy-done.3, bf16[4096,1024]{1,0:T(8,128)(2,1)} %param.14), kind=kOutput, calls=%fused_computation.116 | convolution fusion | flops 4294967296 | bytes 14680064 | tf_op jit(solution)/shard_map/dot_general | solution.py:114
  167.7 4.9 %fusion.24 = bf16[512,256]{0,1:T(8,128)(2,1)} fusion(f32[512,256]{0,1:T(8,128)} %fusion.61, bf16[256,256]{1,0:T(8,128)(2,1)} %get-tuple-element.9, pred[512,256]{1,0:T(32,128)(4,1)S(1)} %copy.44, bf16[512,4096]{1,0:T(8,128)(2,1)} %copy-done.2, bf16[256,4096]{1,0:T(8,128)(2,1)S(1)} %bitcast.121), kind=kOutput, calls=%fused_computation.44 | convolution fusion | flops 1141506048 | bytes 7340032 | tf_op jit(solution)/shard_map/dot_general | solution.py:108
  172.6 3.3 %collective-permute-start.3 = (bf16[512,2,128]{0,2,1:T(8,128)(2,1)}, bf16[512,2,128]{0,2,1:T(8,128)(2,1)}, u32[]{:S(2)}, u32[]{:S(2)}) collective-permute-start(bf16[512,2,128]{0,2,1:T(8,128)(2,1)} %bitcast.126), channel_id=1, source_target_pairs={{0,4},{4,8},{8,12},{12,16},{16,20},{20,24},{24,28},{28,32},{32,36}... | collective-permute-start | bytes 786440 | tf_op jit(solution)/shard_map/ppermute | solution.py:17
  175.9 14.5 %all-gather.5.cloned.1.call-done = bf16[16,16,4096]{2,0,1:T(8,128)(2,1)} async-done(((bf16[16,16,1024]{2,0,1:T(8,128)(2,1)}), bf16[16,16,4096]{2,0,1:T(8,128)(2,1)}) %all-gather.5.cloned.1.call-update) | async-done | bytes 2097168 | tf_op jit(solution)/shard_map/all_gather | solution.py:96
  193.2 6.5 %add_bitcast_fusion = f32[64,8,8,128]{3,1,2,0:T(8,128)} fusion(f32[512,1024]{1,0:T(8,128)} %fusion.63, bf16[256,1024]{1,0:T(8,128)(2,1)} %get-tuple-element.7, pred[512,256]{1,0:T(32,128)(4,1)S(1)} %copy.44, bf16[512,4096]{1,0:T(8,128)(2,1)} %copy-done.2, bf16[256,4096]{1,0:T(8,128)(2,1)S(1)} %bitcast.119), kind=kOutput, calls=%fused_computation.32 | convolution fusion | flops 1343488000 | bytes 11141120 | tf_op jit(solution)/shard_map/dot_general | solution.py:103
  204.2 3.1 %collective-permute-start.2 = (bf16[512,2,128]{0,2,1:T(8,128)(2,1)S(1)}, bf16[512,2,128]{0,2,1:T(8,128)(2,1)S(1)}, u32[]{:S(2)}, u32[]{:S(2)}) collective-permute-start(bf16[512,2,128]{0,2,1:T(8,128)(2,1)S(1)} %bitcast.127), channel_id=1, source_target_pairs={{0,8},{4,12},{8,16},{12,20},{16,24},{20,28},{24,32},{28,36},{32,40... | collective-permute-start | bytes 786440 | tf_op jit(solution)/shard_map/ppermute | solution.py:17
  208.9 5.1 %collective-permute-start.1 = (bf16[512,2,128]{0,2,1:T(8,128)(2,1)S(1)}, bf16[512,2,128]{0,2,1:T(8,128)(2,1)S(1)}, u32[]{:S(2)}, u32[]{:S(2)}) collective-permute-start(bf16[512,2,128]{0,2,1:T(8,128)(2,1)S(1)} %bitcast.128), channel_id=1, source_target_pairs={{0,12},{4,16},{8,20},{12,24},{16,28},{20,32},{24,36},{28,40},{32,4... | collective-permute-start | bytes 786440 | tf_op jit(solution)/shard_map/ppermute | solution.py:17
  215.7 3.8 %collective-permute-start = (bf16[512,2,128]{0,2,1:T(8,128)(2,1)S(1)}, bf16[512,2,128]{0,2,1:T(8,128)(2,1)S(1)}, u32[]{:S(2)}, u32[]{:S(2)}) collective-permute-start(bf16[512,2,128]{0,2,1:T(8,128)(2,1)S(1)} %bitcast.129), channel_id=1, source_target_pairs={{0,16},{4,20},{8,24},{12,28},{16,32},{20,36},{24,40},{28,44},{32,4... | collective-permute-start | bytes 786440 | tf_op jit(solution)/shard_map/ppermute | solution.py:17
  223.5 3.6 %bitcast_dynamic-update-slice_fusion.4 = f32[4,512,2560]{1,2,0:T(8,128)} fusion(bf16[512,4,128]{2,0,1:T(8,128)(2,1)S(1)} %get-tuple-element.14, bf16[512,2,128]{2,0,1:T(8,128)(2,1)} %collective-permute-done.4), kind=kOutput, calls=%fused_computation.24 | convolution fusion | flops 268435456 | bytes 4849664 | tf_op jit(solution)/shard_map/qgd,kd->gqk/dot_general | solution.py:150
  227.1 3.6 %bitcast_dynamic-update-slice_fusion.3 = f32[4,512,2560]{1,2,0:T(8,128)} fusion(f32[4,512,2560]{1,2,0:T(8,128)} %bitcast_dynamic-update-slice_fusion.4, bf16[512,4,128]{2,0,1:T(8,128)(2,1)S(1)} %get-tuple-element.14, bf16[512,2,128]{2,0,1:T(8,128)(2,1)} %collective-permute-done.5), kind=kOutput, calls=%fused_computation.23 | convolution fusion | flops 268435456 | bytes 4849664 | tf_op jit(solution)/shard_map/qgd,kd->gqk/dot_general | solution.py:150
  230.8 3.6 %bitcast_dynamic-update-slice_fusion.2 = f32[4,512,2560]{1,2,0:T(8,128)} fusion(f32[4,512,2560]{1,2,0:T(8,128)} %bitcast_dynamic-update-slice_fusion.3, bf16[512,4,128]{2,0,1:T(8,128)(2,1)S(1)} %get-tuple-element.14, bf16[512,2,128]{2,0,1:T(8,128)(2,1)} %collective-permute-done.6), kind=kOutput, calls=%fused_computation.22 | convolution fusion | flops 268435456 | bytes 4849664 | tf_op jit(solution)/shard_map/qgd,kd->gqk/dot_general | solution.py:150
  234.4 3.7 %bitcast_dynamic-update-slice_fusion.1 = f32[4,512,2560]{1,2,0:T(8,128)} fusion(f32[4,512,2560]{1,2,0:T(8,128)} %bitcast_dynamic-update-slice_fusion.2, bf16[512,4,128]{2,0,1:T(8,128)(2,1)S(1)} %get-tuple-element.14, bf16[512,2,128]{2,0,1:T(8,128)(2,1)} %collective-permute-done.7), kind=kOutput, calls=%fused_computation.21 | convolution fusion | flops 268435456 | bytes 4849664 | tf_op jit(solution)/shard_map/qgd,kd->gqk/dot_general | solution.py:150
  240.8 3.0 %fusion = f32[4,512]{1,0:T(4,128)S(1)} fusion(f32[4,512,2560]{1,2,0:T(8,128)S(1)} %bitcast_dynamic-update-slice_fusion.5, pred[512,2560]{0,1:T(8,128)(4,1)S(1)} %compare_and_fusion), kind=kLoop, calls=%fused_computation.4 | loop fusion | flops 15726592 | bytes 22290432 | tf_op jit(solution)/shard_map/reduce_max | solution.py:157
  243.8 10.6 %fusion.2 = (f32[4,512]{1,0:T(4,128)S(1)}, f32[4,512]{1,0:T(4,128)S(1)}) fusion(f32[4,512,2560]{1,2,0:T(8,128)S(1)} %bitcast_dynamic-update-slice_fusion.5, f32[4,512]{1,0:T(4,128)S(1)} %fusion, pred[512,2560]{0,1:T(8,128)(4,1)S(1)} %compare_and_fusion, f32[4,512,2560]{1,2,0:T(8,128)} %bitcast_dynamic-update-slice_fusion), kind=kLoop, calls=%fused_computation.6 | loop fusion | flops 36696064 | bytes 43278336 | tf_op jit(solution)/shard_map/reduce_sum | solution.py:159
  254.5 9.5 %fusion.4 = f32[4,512]{1,0:T(4,128)S(1)} fusion(f32[4,512,2560]{1,2,0:T(8,128)} %bitcast_dynamic-update-slice_fusion, f32[4,512]{1,0:T(4,128)S(1)} %get-tuple-element.6, pred[512,2560]{0,1:T(8,128)(4,1)S(1)} %compare_and_fusion), kind=kLoop, calls=%fused_computation.8 | loop fusion | flops 20969472 | bytes 22298624 | tf_op jit(solution)/shard_map/reduce_sum | solution.py:159
  265.1 6.5 %divide_convert_fusion.1 = bf16[512,4,128]{0,2,1:T(8,128)(2,1)} fusion(f32[4,512,2560]{1,2,0:T(8,128)S(1)} %bitcast_dynamic-update-slice_fusion.5, f32[4,512]{1,0:T(4,128)S(1)} %fusion, pred[512,2560]{0,1:T(8,128)(4,1)S(1)} %compare_and_fusion, bf16[2560,2,128]{0,2,1:T(8,128)(2,1)S(1)} %constant_dynamic-update-slice_fusion, f32[512,4]{0,1:T(4,128)S(1)} %bitcast.132), kind=kOutput, calls=%fused_computation.50 | convolution fusion | flops 1363673088 | bytes 23478272 | tf_op jit(solution)/shard_map/gqk,kd->qgd/dot_general | solution.py:161
  271.6 10.2 %divide_convert_fusion = bf16[512,4,128]{0,2,1:T(8,128)(2,1)S(1)} fusion(f32[4,512,2560]{1,2,0:T(8,128)} %bitcast_dynamic-update-slice_fusion, f32[4,512]{1,0:T(4,128)S(1)} %get-tuple-element.6, pred[512,2560]{0,1:T(8,128)(4,1)S(1)} %compare_and_fusion, bf16[2560,2,128]{0,2,1:T(8,128)(2,1)} %copy-done.14, f32[512,4]{0,1:T(4,128)S(1)} %bitcast.131), kind=kOutput, calls=%fused_computation.49 | convolution fusion | flops 1363673088 | bytes 23478272 | tf_op jit(solution)/shard_map/gqk,kd->qgd/dot_general | solution.py:161
  (99 shorter events, 42.4 us)
Async XLA Ops:
  6.5 124.7 %copy-start = (bf16[4096,256]{1,0:T(8,128)(2,1)S(1)}, bf16[4096,256]{1,0:T(8,128)(2,1)}, u32[]{:S(2)}) copy-start(bf16[4096,256]{1,0:T(8,128)(2,1)} %param.15) | copy-start | bytes 6291460
  6.5 9.5 %copy-start.16 = (s32[16]{0:T(128)S(1)}, s32[16]{0:T(128)}, u32[]{:S(2)}) copy-start(s32[16]{0:T(128)} %param.21) | copy-start | bytes 196
  6.5 118.9 %all-reduce.3.cloned.1.call-start = ((), (), s32[]{:S(2)}) async-start(), calls=%async_computation.2 | async-start | bytes 3407872 | tf_op jit(solution)/shard_map/psum | solution.py:81
  11.7 113.7 %copy-start.15 = (f32[4096]{0:T(1024)S(1)}, f32[4096]{0:T(1024)}, u32[]{:S(2)}) copy-start(f32[4096]{0:T(1024)} %param.13) | copy-start | bytes 49156
  16.0 149.0 %all-gather.3.cloned.1.call-start = ((), (), s32[]{:S(2)}) async-start(), calls=%async_computation | async-start | bytes 2621440 | tf_op jit(solution)/shard_map/all_gather | solution.py:97
  125.4 65.0 %all-gather.5.cloned.1.call-start = ((), (), s32[]{:S(2)}) async-start(), calls=%async_computation.1 | async-start | bytes 2621440 | tf_op jit(solution)/shard_map/all_gather | solution.py:96
  129.3 1.9 copy-start.2
  134.2 4.9 %copy-start.8 = (f32[512,64]{1,0:T(8,128)}, f32[512,64]{1,0:T(8,128)S(1)}, u32[]{:S(2)}) copy-start(f32[512,64]{1,0:T(8,128)S(1)} %get-tuple-element.21) | copy-start | bytes 393220
  134.2 8.7 %copy-start.10 = (f32[512,64]{1,0:T(8,128)}, f32[512,64]{1,0:T(8,128)S(1)}, u32[]{:S(2)}) copy-start(f32[512,64]{1,0:T(8,128)S(1)} %get-tuple-element.22) | copy-start | bytes 393220
  134.4 1.6 copy-start.6
  136.0 85.1 %collective-permute-start.7 = (bf16[512,2,128]{2,0,1:T(8,128)(2,1)}, bf16[512,2,128]{2,0,1:T(8,128)(2,1)}, u32[]{:S(2)}, u32[]{:S(2)}) collective-permute-start(bf16[512,2,128]{2,0,1:T(8,128)(2,1)} %pad_maximum_fusion.2), channel_id=1, source_target_pairs={{0,4},{4,8},{8,12},{12,16},{16,20},{20,24},{24,28},{28,32},{32,36}... | collective-permute-start | bytes 786440 | tf_op jit(solution)/shard_map/ppermute | solution.py:17
  139.1 76.6 %collective-permute-start.6 = (bf16[512,2,128]{2,0,1:T(8,128)(2,1)}, bf16[512,2,128]{2,0,1:T(8,128)(2,1)}, u32[]{:S(2)}, u32[]{:S(2)}) collective-permute-start(bf16[512,2,128]{2,0,1:T(8,128)(2,1)} %pad_maximum_fusion.2), channel_id=1, source_target_pairs={{0,8},{4,12},{8,16},{12,20},{16,24},{20,28},{24,32},{28,36},{32,40... | collective-permute-start | bytes 786440 | tf_op jit(solution)/shard_map/ppermute | solution.py:17
  142.9 66.0 %collective-permute-start.5 = (bf16[512,2,128]{2,0,1:T(8,128)(2,1)}, bf16[512,2,128]{2,0,1:T(8,128)(2,1)}, u32[]{:S(2)}, u32[]{:S(2)}) collective-permute-start(bf16[512,2,128]{2,0,1:T(8,128)(2,1)} %pad_maximum_fusion.2), channel_id=1, source_target_pairs={{0,12},{4,16},{8,20},{12,24},{16,28},{20,32},{24,36},{28,40},{32,4... | collective-permute-start | bytes 786440 | tf_op jit(solution)/shard_map/ppermute | solution.py:17
  147.9 56.3 %collective-permute-start.4 = (bf16[512,2,128]{2,0,1:T(8,128)(2,1)}, bf16[512,2,128]{2,0,1:T(8,128)(2,1)}, u32[]{:S(2)}, u32[]{:S(2)}) collective-permute-start(bf16[512,2,128]{2,0,1:T(8,128)(2,1)} %pad_maximum_fusion.2), channel_id=1, source_target_pairs={{0,16},{4,20},{8,24},{12,28},{16,32},{20,36},{24,40},{28,44},{32,4... | collective-permute-start | bytes 786440 | tf_op jit(solution)/shard_map/ppermute | solution.py:17
  150.2 6.5 %copy-start.3 = (bf16[512,4096]{1,0:T(8,128)(2,1)S(1)}, bf16[512,4096]{1,0:T(8,128)(2,1)}, u32[]{:S(2)}) copy-start(bf16[512,4096]{1,0:T(8,128)(2,1)} %copy-done.2) | copy-start | bytes 12582916
  172.6 91.5 %collective-permute-start.3 = (bf16[512,2,128]{0,2,1:T(8,128)(2,1)}, bf16[512,2,128]{0,2,1:T(8,128)(2,1)}, u32[]{:S(2)}, u32[]{:S(2)}) collective-permute-start(bf16[512,2,128]{0,2,1:T(8,128)(2,1)} %bitcast.126), channel_id=1, source_target_pairs={{0,4},{4,8},{8,12},{12,16},{16,20},{20,24},{24,28},{28,32},{32,36}... | collective-permute-start | bytes 786440 | tf_op jit(solution)/shard_map/ppermute | solution.py:17
  204.2 59.9 %collective-permute-start.2 = (bf16[512,2,128]{0,2,1:T(8,128)(2,1)S(1)}, bf16[512,2,128]{0,2,1:T(8,128)(2,1)S(1)}, u32[]{:S(2)}, u32[]{:S(2)}) collective-permute-start(bf16[512,2,128]{0,2,1:T(8,128)(2,1)S(1)} %bitcast.127), channel_id=1, source_target_pairs={{0,8},{4,12},{8,16},{12,20},{16,24},{20,28},{24,32},{28,36},{32,40... | collective-permute-start | bytes 786440 | tf_op jit(solution)/shard_map/ppermute | solution.py:17
  208.9 55.1 %collective-permute-start.1 = (bf16[512,2,128]{0,2,1:T(8,128)(2,1)S(1)}, bf16[512,2,128]{0,2,1:T(8,128)(2,1)S(1)}, u32[]{:S(2)}, u32[]{:S(2)}) collective-permute-start(bf16[512,2,128]{0,2,1:T(8,128)(2,1)S(1)} %bitcast.128), channel_id=1, source_target_pairs={{0,12},{4,16},{8,20},{12,24},{16,28},{20,32},{24,36},{28,40},{32,4... | collective-permute-start | bytes 786440 | tf_op jit(solution)/shard_map/ppermute | solution.py:17
  215.7 7.1 %copy-start.5 = (bf16[512,2,64]{2,0,1:T(8,128)(2,1)S(1)}, bf16[512,2,64]{2,0,1:T(8,128)(2,1)}, u32[]{:S(2)}) copy-start(bf16[512,2,64]{2,0,1:T(8,128)(2,1)} %copy-done.4) | copy-start | bytes 393220
  215.7 7.1 %copy-start.7 = (bf16[512,2,64]{2,0,1:T(8,128)(2,1)S(1)}, bf16[512,2,64]{2,0,1:T(8,128)(2,1)}, u32[]{:S(2)}) copy-start(bf16[512,2,64]{2,0,1:T(8,128)(2,1)} %copy-done.6) | copy-start | bytes 393220
  215.7 48.2 %collective-permute-start = (bf16[512,2,128]{0,2,1:T(8,128)(2,1)S(1)}, bf16[512,2,128]{0,2,1:T(8,128)(2,1)S(1)}, u32[]{:S(2)}, u32[]{:S(2)}) collective-permute-start(bf16[512,2,128]{0,2,1:T(8,128)(2,1)S(1)} %bitcast.129), channel_id=1, source_target_pairs={{0,16},{4,20},{8,24},{12,28},{16,32},{20,36},{24,40},{28,44},{32,4... | collective-permute-start | bytes 786440 | tf_op jit(solution)/shard_map/ppermute | solution.py:17
  265.1 6.5 %copy-start.14 = (bf16[2560,2,128]{0,2,1:T(8,128)(2,1)}, bf16[2560,2,128]{0,2,1:T(8,128)(2,1)S(1)}, u32[]{:S(2)}) copy-start(bf16[2560,2,128]{0,2,1:T(8,128)(2,1)S(1)} %constant_dynamic-update-slice_fusion) | copy-start | bytes 3932164
  271.6 10.2 %copy-start.12 = (bf16[512,4,128]{0,2,1:T(8,128)(2,1)S(1)}, bf16[512,4,128]{0,2,1:T(8,128)(2,1)}, u32[]{:S(2)}) copy-start(bf16[512,4,128]{0,2,1:T(8,128)(2,1)} %divide_convert_fusion.1) | copy-start | bytes 1572868
  271.6 11.6 %copy-start.1 = (bf16[4096,256]{1,0:T(8,128)(2,1)S(1)}, bf16[4096,256]{1,0:T(8,128)(2,1)}, u32[]{:S(2)}) copy-start(bf16[4096,256]{1,0:T(8,128)(2,1)} %param.15) | copy-start | bytes 6291460
  (4 other events, 4.1 us)
Sparse Core Ops, SparseCore 0:
  16.1 109.2 all-reduce.2
  127.1 30.7 all-gather.2
  159.5 30.9 all-gather.4
where the time goes:
time: 291 us; the launch traced here: 290 us
  waiting for transfers between devices  121 us (42%)
  matrix products  73.8 us (25%)
  other arithmetic  36.3 us (12%)
  starting transfers between devices  29.2 us (10%)
  local copies, waits for them, and re-layouts  16.2 us (6%)
  between operations  13.6 us (5%)
    psum x1, waiting for transfers between devices, body(): lax.psum(selector(query_up_maps).astype(jnp.bfloat16), 'tok')  106 us
    ppermute x8, starting transfers between devices, from_behind(): return lax.ppermute(x, axis, pairs)  29.2 us
    dot_general x10, matrix products, dense_scores(): jnp.einsum('qgd,kd->gqk', q_group, block_keys, preferred_element_type=jnp...  24.5 us
    reduce_sum x2, other arithmetic, body(): totals = jnp.sum(weights, axis=-1)  20.2 us
    dot_general x2, matrix products, body(): jnp.einsum('gqk,kd->qgd', probs, all_values[:, kv_group, :], preferred_el...  16.6 us
    all_gather x1, waiting for transfers between devices, body(): lax.all_gather(query_down_table, 'mlp', axis=2, tiled=True)  14.5 us
    dot_general x1, matrix products, body(): jnp.dot(normed_input, query_weight, preferred_element_type=jnp.float32)  8.29 us
    dot_general x4, matrix products, selector(): jnp.einsum('th,hrc->trc', picker, stored, preferred_element_type=jnp.floa...  6.56 us
  transfers between devices with their start and end apart: 11, of which 2 were waited for; matrix products, arithmetic and copies ran while one was open for 33% of the time, Pallas kernels for 0%

commit v1 on v0

--- a/solution.py
+++ b/solution.py
@@ -78,7 +78,9 @@
     summed = (
         lax.psum(selector(query_down_maps).astype(jnp.bfloat16), "tok").astype(jnp.float32),
         lax.psum(selector(value_down_maps).astype(jnp.bfloat16), "tok").astype(jnp.float32),
-        lax.psum(selector(query_up_maps).astype(jnp.bfloat16), "tok").astype(jnp.float32),
+        jnp.sum(lax.all_gather(selector(query_up_maps).astype(jnp.bfloat16), "tok"), axis=0).astype(
+            jnp.float32
+        ),
         lax.psum(selector(value_up_maps).astype(jnp.bfloat16), "tok").astype(jnp.float32),
     )
     query_down_table = summed[0].astype(jnp.bfloat16)

time: 291 us -> 365 us (1.25)
  waiting for transfers between devices: 121 us -> 179 us
  other arithmetic: 36.3 us -> 45.1 us
  local copies, waits for them, and re-layouts: 16.2 us -> 24 us
    all_gather x0 -> x1, waiting for transfers between devices: none -> 58.7 us  [body(): lax.all_gather(selector(query_up_maps).astype(jnp.bfloat16), 'tok')]
    reduce_sum x0 -> x1, other arithmetic: none -> 9.96 us  [body(): jnp.sum(lax.all_gather(selector(query_up_maps).astype(jnp.bfloat16), 'tok...]
    unnamed x41 -> x45, local copies, waits for them, and re-layouts: 6.52 us -> 11.6 us
  transfers between devices with their start and end apart: 11 -> 12, of which waited for: 2 -> 3; matrix products, arithmetic and copies ran while one was open for 33% -> 19% of each run, Pallas kernels for 0% -> 0%
where the time goes in v1:
time: 365 us; the launch traced here: 364 us
  waiting for transfers between devices  179 us (49%)
  matrix products  73.7 us (20%)
  other arithmetic  45.1 us (12%)
  starting transfers between devices  28.7 us (8%)
  local copies, waits for them, and re-layouts  24 us (7%)
  between operations  13.6 us (4%)
    psum x1, waiting for transfers between devices, body(): lax.psum(selector(query_down_maps).astype(jnp.bfloat16), 'tok')  108 us
    all_gather x1, waiting for transfers between devices, body(): lax.all_gather(selector(query_up_maps).astype(jnp.bfloat16), 'tok')  58.7 us
    ppermute x8, starting transfers between devices, from_behind(): return lax.ppermute(x, axis, pairs)  28.6 us
    dot_general x10, matrix products, dense_scores(): jnp.einsum('qgd,kd->gqk', q_group, block_keys, preferred_element_type=jnp...  24.6 us
    reduce_sum x2, other arithmetic, body(): totals = jnp.sum(weights, axis=-1)  20.4 us
    dot_general x2, matrix products, body(): jnp.einsum('gqk,kd->qgd', probs, all_values[:, kv_group, :], preferred_el...  17.8 us
    unnamed x45, local copies, waits for them, and re-layouts  11.6 us
    all_gather x1, waiting for transfers between devices, body(): lax.all_gather(query_down_table, 'mlp', axis=2, tiled=True)  11 us
  transfers between devices with their start and end apart: 12, of which 3 were waited for; matrix products, arithmetic and copies ran while one was open for 19% of the time, Pallas kernels for 0%

profile of v1, /device:TPU:1, one launch (start us, length us, event | category | flops | bytes accessed | tf_op | source)
XLA Modules:
  0.0 364.0 jit_solution(2617427261857559917)
XLA Ops:
  13.6 108.3 %all-reduce.3.cloned.1.call-done = (bf16[16,16,1024]{2,0,1:T(8,128)(2,1)}, bf16[256,256]{1,0:T(8,128)(2,1)}, bf16[16,16,1024]{2,0,1:T(8,128)(2,1)}) async-done(((bf16[16,16,1024]{2,0,1:T(8,128)(2,1)}, bf16[256,256]{1,0:T(8,128)(2,1)}, bf16[16,16,1024]{2,0,1:T(8,128)(2,1)}), (bf16[16,16,1024]{2,0,1:T(8,128)(2,1)}, bf16[256,256]{1,0:T(8,128)(2,1)}, ...) | async-done | bytes 1179664 | tf_op jit(solution)/shard_map/psum | solution.py:79
  124.2 3.2 fusion.12
  136.0 3.1 collective-permute-start.7
  139.1 3.8 %collective-permute-start.6 = (bf16[512,2,128]{2,0,1:T(8,128)(2,1)}, bf16[512,2,128]{2,0,1:T(8,128)(2,1)}, u32[]{:S(2)}, u32[]{:S(2)}) collective-permute-start(bf16[512,2,128]{2,0,1:T(8,128)(2,1)} %pad_maximum_fusion.2), channel_id=1, source_target_pairs={{0,8},{4,12},{8,16},{12,20},{16,24},{20,28},{24,32},{28,36},{32,40... | collective-permute-start | bytes 786440 | tf_op jit(solution)/shard_map/ppermute | solution.py:17
  143.2 4.4 %fusion.61 = f32[512,256]{0,1:T(8,128)S(1)} fusion(bf16[512,4096]{1,0:T(8,128)(2,1)} %copy-done.3, bf16[4096,256]{1,0:T(8,128)(2,1)} %param.16), kind=kOutput, calls=%fused_computation.114 | convolution fusion | flops 1073741824 | bytes 6815744 | tf_op jit(solution)/shard_map/dot_general | solution.py:125
  147.6 8.3 %fusion.63 = f32[512,1024]{1,0:T(8,128)} fusion(bf16[512,4096]{1,0:T(8,128)(2,1)S(1)} %copy-done.4, bf16[4096,1024]{1,0:T(8,128)(2,1)} %param.14), kind=kOutput, calls=%fused_computation.116 | convolution fusion | flops 4294967296 | bytes 14680064 | tf_op jit(solution)/shard_map/dot_general | solution.py:116
  158.7 4.4 %fusion.24 = bf16[512,256]{0,1:T(8,128)(2,1)} fusion(f32[512,256]{0,1:T(8,128)S(1)} %fusion.61, bf16[256,256]{1,0:T(8,128)(2,1)S(1)} %copy-done.18, pred[512,256]{1,0:T(32,128)(4,1)S(1)} %copy.78, bf16[512,4096]{1,0:T(8,128)(2,1)} %copy-done.3, bf16[256,4096]{1,0:T(8,128)(2,1)S(1)} %bitcast.124), kind=kOutput, calls=%fused_computation.44 | convolution fusion | flops 1141506048 | bytes 7340032 | tf_op jit(solution)/shard_map/dot_general | solution.py:110
  163.1 4.5 %collective-permute-start.2 = (bf16[512,2,128]{0,2,1:T(8,128)(2,1)}, bf16[512,2,128]{0,2,1:T(8,128)(2,1)}, u32[]{:S(2)}, u32[]{:S(2)}) collective-permute-start(bf16[512,2,128]{0,2,1:T(8,128)(2,1)} %bitcast.5), channel_id=1, source_target_pairs={{0,8},{4,12},{8,16},{12,20},{16,24},{20,28},{24,32},{28,36},{32,40... | collective-permute-start | bytes 786440 | tf_op jit(solution)/shard_map/ppermute | solution.py:17
  170.6 3.4 collective-permute-start
  176.0 11.0 %all-gather.7.cloned.1.call-done = bf16[16,16,4096]{2,0,1:T(8,128)(2,1)} async-done(((bf16[16,16,1024]{2,0,1:T(8,128)(2,1)}), bf16[16,16,4096]{2,0,1:T(8,128)(2,1)}) %all-gather.7.cloned.1.call-update) | async-done | bytes 2097168 | tf_op jit(solution)/shard_map/all_gather | solution.py:98
  189.8 3.7 %collective-permute-start.3 = (bf16[512,2,128]{0,2,1:T(8,128)(2,1)}, bf16[512,2,128]{0,2,1:T(8,128)(2,1)S(1)}, u32[]{:S(2)}, u32[]{:S(2)}) collective-permute-start(bf16[512,2,128]{0,2,1:T(8,128)(2,1)} %bitcast.5), channel_id=1, source_target_pairs={{0,4},{4,8},{8,12},{12,16},{16,20},{20,24},{24,28},{28,32},{32,36}... | collective-permute-start | bytes 786440 | tf_op jit(solution)/shard_map/ppermute | solution.py:17
  195.2 4.1 %collective-permute-start.5 = (bf16[512,2,128]{2,0,1:T(8,128)(2,1)}, bf16[512,2,128]{2,0,1:T(8,128)(2,1)}, u32[]{:S(2)}, u32[]{:S(2)}) collective-permute-start(bf16[512,2,128]{2,0,1:T(8,128)(2,1)} %pad_maximum_fusion.2), channel_id=1, source_target_pairs={{0,12},{4,16},{8,20},{12,24},{16,28},{20,32},{24,36},{28,40},{32,4... | collective-permute-start | bytes 786440 | tf_op jit(solution)/shard_map/ppermute | solution.py:17
  201.0 3.1 collective-permute-start.4
  208.3 58.7 %all-gather.9.cloned.1.call-done = bf16[512,16,1024]{2,0,1:T(8,128)(2,1)} async-done(((bf16[16,16,1024]{2,0,1:T(8,128)(2,1)}), bf16[512,16,1024]{2,0,1:T(8,128)(2,1)}) %all-gather.9.cloned.1.call-update) | async-done | bytes 16777232 | tf_op jit(solution)/shard_map/all_gather | solution.py:81
  267.1 10.0 %reduce_sum.70 = bf16[16,16,1024]{2,0,1:T(8,128)(2,1)} reduce(bf16[32,16,16,1024]{3,1,0,2:T(8,128)(2,1)} %bitcast.120, bf16[]{:T(256)} %constant.35.clone.1), dimensions={0}, to_apply=%region_8.9 | reduce | flops 8126464 | bytes 17301506 | tf_op jit(solution)/shard_map/reduce_sum | solution.py:81
  279.2 6.5 %add_bitcast_fusion = f32[64,8,8,128]{3,1,2,0:T(8,128)} fusion(f32[512,1024]{1,0:T(8,128)} %fusion.63, bf16[256,1024]{1,0:T(8,128)(2,1)} %bitcast.123, pred[512,256]{1,0:T(32,128)(4,1)S(1)} %copy.78, bf16[512,4096]{1,0:T(8,128)(2,1)} %copy-done.3, bf16[256,4096]{1,0:T(8,128)(2,1)S(1)} %bitcast.121), kind=kOutput, calls=%fused_computation.32 | convolution fusion | flops 1343488000 | bytes 11141120 | tf_op jit(solution)/shard_map/dot_general | solution.py:105
  297.5 3.6 bitcast_dynamic-update-slice_fusion.4
  301.1 3.6 bitcast_dynamic-update-slice_fusion.3
  304.7 3.7 %bitcast_dynamic-update-slice_fusion.2 = f32[4,512,2560]{1,2,0:T(8,128)} fusion(f32[4,512,2560]{1,2,0:T(8,128)} %bitcast_dynamic-update-slice_fusion.3, bf16[512,4,128]{2,0,1:T(8,128)(2,1)S(1)} %get-tuple-element.13, bf16[512,2,128]{2,0,1:T(8,128)(2,1)} %collective-permute-done.6), kind=kOutput, calls=%fused_computation.22 | convolution fusion | flops 268435456 | bytes 4849664 | tf_op jit(solution)/shard_map/qgd,kd->gqk/dot_general | solution.py:152
  308.4 3.7 %bitcast_dynamic-update-slice_fusion.1 = f32[4,512,2560]{1,2,0:T(8,128)} fusion(f32[4,512,2560]{1,2,0:T(8,128)} %bitcast_dynamic-update-slice_fusion.2, bf16[512,4,128]{2,0,1:T(8,128)(2,1)S(1)} %get-tuple-element.13, bf16[512,2,128]{2,0,1:T(8,128)(2,1)} %collective-permute-done.7), kind=kOutput, calls=%fused_computation.21 | convolution fusion | flops 268435456 | bytes 4849664 | tf_op jit(solution)/shard_map/qgd,kd->gqk/dot_general | solution.py:152
  317.8 10.9 %fusion.2 = (f32[4,512]{1,0:T(4,128)S(1)}, f32[4,512]{1,0:T(4,128)S(1)}) fusion(f32[4,512,2560]{1,2,0:T(8,128)S(1)} %bitcast_dynamic-update-slice_fusion.5, f32[4,512]{1,0:T(4,128)S(1)} %fusion, pred[512,2560]{0,1:T(8,128)(4,1)S(1)} %compare_and_fusion, f32[4,512,2560]{1,2,0:T(8,128)} %bitcast_dynamic-update-slice_fusion), kind=kLoop, calls=%fused_computation.6 | loop fusion | flops 36696064 | bytes 43278336 | tf_op jit(solution)/shard_map/reduce_sum | solution.py:161
  328.7 9.5 %fusion.4 = f32[4,512]{1,0:T(4,128)S(1)} fusion(f32[4,512,2560]{1,2,0:T(8,128)} %bitcast_dynamic-update-slice_fusion, f32[4,512]{1,0:T(4,128)S(1)} %get-tuple-element.6, pred[512,2560]{0,1:T(8,128)(4,1)S(1)} %compare_and_fusion), kind=kLoop, calls=%fused_computation.8 | loop fusion | flops 20969472 | bytes 22298624 | tf_op jit(solution)/shard_map/reduce_sum | solution.py:161
  338.2 7.6 %divide_convert_fusion.1 = bf16[512,4,128]{0,2,1:T(8,128)(2,1)} fusion(f32[4,512,2560]{1,2,0:T(8,128)S(1)} %bitcast_dynamic-update-slice_fusion.5, f32[4,512]{1,0:T(4,128)S(1)} %fusion, pred[512,2560]{0,1:T(8,128)(4,1)S(1)} %compare_and_fusion, bf16[2560,2,128]{0,2,1:T(8,128)(2,1)} %constant_dynamic-update-slice_fusion, f32[512,4]{0,1:T(4,128)S(1)} %bitcast.129), kind=kOutput, calls=%fused_computation.50 | convolution fusion | flops 1363673088 | bytes 23478272 | tf_op jit(solution)/shard_map/gqk,kd->qgd/dot_general | solution.py:163
  345.9 10.1 %divide_convert_fusion = bf16[512,4,128]{0,2,1:T(8,128)(2,1)S(1)} fusion(f32[4,512,2560]{1,2,0:T(8,128)} %bitcast_dynamic-update-slice_fusion, f32[4,512]{1,0:T(4,128)S(1)} %get-tuple-element.6, pred[512,2560]{0,1:T(8,128)(4,1)S(1)} %compare_and_fusion, bf16[2560,2,128]{0,2,1:T(8,128)(2,1)} %constant_dynamic-update-slice_fusion, f32[512,4]{0,1:T(4,128)S(1)} %bitcast.128), kind=kOutput, calls=%fused_computation.49 | convolution fusion | flops 1363673088 | bytes 23478272 | tf_op jit(solution)/shard_map/gqk,kd->qgd/dot_general | solution.py:163
  (107 shorter events, 57.1 us)
Async XLA Ops:
  6.5 124.7 %copy-start = (bf16[4096,256]{1,0:T(8,128)(2,1)S(1)}, bf16[4096,256]{1,0:T(8,128)(2,1)}, u32[]{:S(2)}) copy-start(bf16[4096,256]{1,0:T(8,128)(2,1)} %param.15) | copy-start | bytes 6291460
  6.5 116.2 %copy-start.14 = (bf16[8,16,1024]{2,1,0:T(8,128)(2,1)S(1)}, bf16[8,16,1024]{2,1,0:T(8,128)(2,1)}, u32[]{:S(2)}) copy-start(bf16[8,16,1024]{2,1,0:T(8,128)(2,1)} %param.19) | copy-start | bytes 786436
  6.5 117.4 %copy-start.17 = (s32[16]{0:T(128)S(1)}, s32[16]{0:T(128)}, u32[]{:S(2)}) copy-start(s32[16]{0:T(128)} %param.21) | copy-start | bytes 196
  6.5 115.4 %all-reduce.3.cloned.1.call-start = ((), (), s32[]{:S(2)}) async-start(), calls=%async_computation.3 | async-start | bytes 2359296 | tf_op jit(solution)/shard_map/psum | solution.py:79
  11.4 116.0 %copy-start.16 = (f32[4096]{0:T(1024)S(1)}, f32[4096]{0:T(1024)}, u32[]{:S(2)}) copy-start(f32[4096]{0:T(1024)} %param.13) | copy-start | bytes 49156
  13.6 142.3 %all-gather.5.cloned.1.call-start = ((), (), s32[]{:S(2)}) async-start(), calls=%async_computation | async-start | bytes 2621440 | tf_op jit(solution)/shard_map/all_gather | solution.py:99
  122.0 65.0 %all-gather.7.cloned.1.call-start = ((), (), s32[]{:S(2)}) async-start(), calls=%async_computation.1 | async-start | bytes 2621440 | tf_op jit(solution)/shard_map/all_gather | solution.py:98
  122.7 144.3 %all-gather.9.cloned.1.call-start = ((), (), s32[]{:S(2)}) async-start(), calls=%async_computation.2 | async-start | bytes 17301504 | tf_op jit(solution)/shard_map/all_gather | solution.py:81
  124.2 3.5 copy-start.2
  133.3 14.3 %copy-start.15 = (s32[512]{0:T(512)}, s32[512]{0:T(512)S(1)}, u32[]{:S(2)}) copy-start(s32[512]{0:T(512)S(1)} %select_reduce_fusion) | copy-start | bytes 6148
  134.3 4.8 %copy-start.9 = (f32[512,64]{1,0:T(8,128)}, f32[512,64]{1,0:T(8,128)S(1)}, u32[]{:S(2)}) copy-start(f32[512,64]{1,0:T(8,128)S(1)} %get-tuple-element.20) | copy-start | bytes 393220
  134.3 4.8 %copy-start.11 = (f32[512,64]{1,0:T(8,128)}, f32[512,64]{1,0:T(8,128)S(1)}, u32[]{:S(2)}) copy-start(f32[512,64]{1,0:T(8,128)S(1)} %get-tuple-element.21) | copy-start | bytes 393220
  136.0 159.1 %collective-permute-start.7 = (bf16[512,2,128]{2,0,1:T(8,128)(2,1)}, bf16[512,2,128]{2,0,1:T(8,128)(2,1)}, u32[]{:S(2)}, u32[]{:S(2)}) collective-permute-start(bf16[512,2,128]{2,0,1:T(8,128)(2,1)} %pad_maximum_fusion.2), channel_id=1, source_target_pairs={{0,4},{4,8},{8,12},{12,16},{16,20},{20,24},{24,28},{28,32},{32,36}... | collective-permute-start | bytes 786440 | tf_op jit(solution)/shard_map/ppermute | solution.py:17
  139.1 154.3 %collective-permute-start.6 = (bf16[512,2,128]{2,0,1:T(8,128)(2,1)}, bf16[512,2,128]{2,0,1:T(8,128)(2,1)}, u32[]{:S(2)}, u32[]{:S(2)}) collective-permute-start(bf16[512,2,128]{2,0,1:T(8,128)(2,1)} %pad_maximum_fusion.2), channel_id=1, source_target_pairs={{0,8},{4,12},{8,16},{12,20},{16,24},{20,28},{24,32},{28,36},{32,40... | collective-permute-start | bytes 786440 | tf_op jit(solution)/shard_map/ppermute | solution.py:17
  143.2 4.4 %copy-start.4 = (bf16[512,4096]{1,0:T(8,128)(2,1)S(1)}, bf16[512,4096]{1,0:T(8,128)(2,1)}, u32[]{:S(2)}) copy-start(bf16[512,4096]{1,0:T(8,128)(2,1)} %copy-done.3) | copy-start | bytes 12582916
  163.1 37.9 %collective-permute-start.2 = (bf16[512,2,128]{0,2,1:T(8,128)(2,1)}, bf16[512,2,128]{0,2,1:T(8,128)(2,1)}, u32[]{:S(2)}, u32[]{:S(2)}) collective-permute-start(bf16[512,2,128]{0,2,1:T(8,128)(2,1)} %bitcast.5), channel_id=1, source_target_pairs={{0,8},{4,12},{8,16},{12,20},{16,24},{20,28},{24,32},{28,36},{32,40... | collective-permute-start | bytes 786440 | tf_op jit(solution)/shard_map/ppermute | solution.py:17
  167.6 27.6 %collective-permute-start.1 = (bf16[512,2,128]{0,2,1:T(8,128)(2,1)}, bf16[512,2,128]{0,2,1:T(8,128)(2,1)}, u32[]{:S(2)}, u32[]{:S(2)}) collective-permute-start(bf16[512,2,128]{0,2,1:T(8,128)(2,1)} %bitcast.5), channel_id=1, source_target_pairs={{0,12},{4,16},{8,20},{12,24},{16,28},{20,32},{24,36},{28,40},{32,4... | collective-permute-start | bytes 786440 | tf_op jit(solution)/shard_map/ppermute | solution.py:17
  170.6 19.2 %collective-permute-start = (bf16[512,2,128]{0,2,1:T(8,128)(2,1)}, bf16[512,2,128]{0,2,1:T(8,128)(2,1)}, u32[]{:S(2)}, u32[]{:S(2)}) collective-permute-start(bf16[512,2,128]{0,2,1:T(8,128)(2,1)} %bitcast.5), channel_id=1, source_target_pairs={{0,16},{4,20},{8,24},{12,28},{16,32},{20,36},{24,40},{28,44},{32,4... | collective-permute-start | bytes 786440 | tf_op jit(solution)/shard_map/ppermute | solution.py:17
  189.8 16.1 %collective-permute-start.3 = (bf16[512,2,128]{0,2,1:T(8,128)(2,1)}, bf16[512,2,128]{0,2,1:T(8,128)(2,1)S(1)}, u32[]{:S(2)}, u32[]{:S(2)}) collective-permute-start(bf16[512,2,128]{0,2,1:T(8,128)(2,1)} %bitcast.5), channel_id=1, source_target_pairs={{0,4},{4,8},{8,12},{12,16},{16,20},{20,24},{24,28},{28,32},{32,36}... | collective-permute-start | bytes 786440 | tf_op jit(solution)/shard_map/ppermute | solution.py:17
  195.2 96.6 %collective-permute-start.5 = (bf16[512,2,128]{2,0,1:T(8,128)(2,1)}, bf16[512,2,128]{2,0,1:T(8,128)(2,1)}, u32[]{:S(2)}, u32[]{:S(2)}) collective-permute-start(bf16[512,2,128]{2,0,1:T(8,128)(2,1)} %pad_maximum_fusion.2), channel_id=1, source_target_pairs={{0,12},{4,16},{8,20},{12,24},{16,28},{20,32},{24,36},{28,40},{32,4... | collective-permute-start | bytes 786440 | tf_op jit(solution)/shard_map/ppermute | solution.py:17
  201.0 89.1 %collective-permute-start.4 = (bf16[512,2,128]{2,0,1:T(8,128)(2,1)}, bf16[512,2,128]{2,0,1:T(8,128)(2,1)}, u32[]{:S(2)}, u32[]{:S(2)}) collective-permute-start(bf16[512,2,128]{2,0,1:T(8,128)(2,1)} %pad_maximum_fusion.2), channel_id=1, source_target_pairs={{0,16},{4,20},{8,24},{12,28},{16,32},{20,36},{24,40},{28,44},{32,4... | collective-permute-start | bytes 786440 | tf_op jit(solution)/shard_map/ppermute | solution.py:17
  293.4 3.3 copy-start.6
  345.9 10.2 %copy-start.13 = (bf16[512,4,128]{0,2,1:T(8,128)(2,1)S(1)}, bf16[512,4,128]{0,2,1:T(8,128)(2,1)}, u32[]{:S(2)}) copy-start(bf16[512,4,128]{0,2,1:T(8,128)(2,1)} %divide_convert_fusion.1) | copy-start | bytes 1572868
  345.9 11.6 %copy-start.1 = (bf16[4096,256]{1,0:T(8,128)(2,1)S(1)}, bf16[4096,256]{1,0:T(8,128)(2,1)}, u32[]{:S(2)}) copy-start(bf16[4096,256]{1,0:T(8,128)(2,1)} %param.15) | copy-start | bytes 6291460
  (7 other events, 12.4 us)
Sparse Core Ops, SparseCore 0:
  13.7 108.2 all-reduce.2
  123.6 30.7 all-gather.4
  156.1 30.9 all-gather.6
  189.2 77.8 all-gather.8
